TPU v7x, 32 devices: a whole 2x2x4 slice. The times are simulated.
32 devices in a mesh: ctx: 8 (over z, x), ch: 4 (over y, core).
Axes of the slice: x: 2, y: 2, z: 4, core: 2. Of those that a mesh axis runs over, the one named last changes fastest.
Arguments:
- query_input: bfloat16 [4096, 4096], P('ch', 'ctx'), may hold values from -6 to 6
- key_input: bfloat16 [4096, 4096], P('ch', 'ctx'), may hold values from -6 to 6
- value_input: bfloat16 [4096, 4096], P('ch', 'ctx'), may hold values from -6 to 6
- decay_rate: float32 [8, 16], P('ch'), may hold values from 0 to 1, as said below
- residue: float32 [8, 16], P('ch'), may hold values from -1 to 1
- doc_ends: int32 [4], replicated, may hold values from 1 to 4096, as said below
- out_weight: bfloat16 [4096, 4096], P(None, 'ch'), may hold values from -0.09375 to 0.09375
- out_cotangent: bfloat16 [4096, 4096], P('ctx', 'ch'), may hold values from -6 to 6
Outputs:
- query_grad: bfloat16 [4096, 4096], P('ch', 'ctx')
- key_grad: bfloat16 [4096, 4096], P('ch', 'ctx')
- value_grad: bfloat16 [4096, 4096], P('ch', 'ctx')
- weight_grad: float32 [4096, 4096], P('ctx', 'ch')
Inputs may be any that keep to these rules, and one draw needn't show every extreme that they name: `doc_ends`: strictly increasing; the last entry equals 4096. `decay_rate`: positive.
All inputs are finite; a program needn't handle non-finite values.
Results may differ from a plain program's by a relative error of at most 0.0029.
Values may be sent and summed in bfloat16 or wider, within the bound.
A program may use at most 128 MiB of HBM per device.

v0:
```python
import math
import jax
import jax.numpy as jnp
from jax import lax
from jax.sharding import PartitionSpec as P

HIGH = lax.Precision.HIGH
TILE = 128


def doc_of(doc_ends, positions):
    return jnp.sum((doc_ends[None, :] <= positions[:, None]).astype(jnp.int32), axis=1)


def local_kernel(decay_rate, residue, doc_ids, length):
    groups = decay_rate.shape[0]
    place = jnp.arange(length, dtype=jnp.float32)
    narrow = jnp.arange(TILE, dtype=jnp.float32)
    half = 0.5 * TILE
    rising = jnp.exp(-decay_rate[:, None, :] * (place - half)[None, :, None]) * residue[:, None, :]
    falling = jnp.exp(decay_rate[:, None, :] * (narrow - half)[None, :, None])
    strip = jnp.einsum("gtn,gsn->gts", rising, falling, precision=lax.Precision.HIGHEST)
    columns = []
    for start in range(0, length, TILE):
        top = jnp.zeros((groups, start, TILE), jnp.float32)
        columns.append(jnp.concatenate([top, strip[:, : length - start]], axis=1))
    kernel = jnp.concatenate(columns, axis=2)
    offsets = jnp.arange(length, dtype=jnp.int32)
    causal = (offsets[:, None] >= offsets[None, :]) & (doc_ids[:, None] == doc_ids[None, :])
    return jnp.where(causal[None], kernel, 0.0)


def exchange_rows(gated, n_ctx, n_ch):
    rows, length = gated.shape
    mine = rows * n_ch // n_ctx
    pieces = gated.reshape(n_ctx // n_ch, n_ch, mine // n_ch, length)
    pieces = lax.all_to_all(pieces, "ch", split_axis=1, concat_axis=0, tiled=True)
    pieces = pieces.reshape(n_ctx, mine // n_ch, length)
    pieces = lax.all_to_all(pieces, "ctx", split_axis=0, concat_axis=0, tiled=True)
    pieces = pieces.transpose(1, 0, 2).reshape(mine // n_ch, n_ctx * length)
    return lax.all_gather(pieces, "ch", axis=0, tiled=True)


def local(
    query_input, key_input, value_input, decay_rate, residue, doc_ends, out_weight, out_cotangent
):
    rows_here, length = query_input.shape
    n_ctx, n_ch = (lax.axis_size("ctx"), lax.axis_size("ch"))
    groups = decay_rate.shape[0]
    group_rows = rows_here // groups
    me = lax.axis_index("ctx")
    offsets = jnp.arange(length, dtype=jnp.int32)
    place = offsets.astype(jnp.float32)
    doc_ids = doc_of(doc_ends, me * length + offsets)
    blocks = jnp.arange(n_ctx, dtype=jnp.int32)
    last_ids = doc_of(doc_ends, (blocks + 1) * length - 1)
    previous = jnp.where(me > 0, jnp.sum((doc_ends <= me * length - 1).astype(jnp.int32)), -1)
    last = doc_ids[-1]
    cotangent_all = lax.all_gather(out_cotangent, "ctx", axis=0, tiled=True)
    alive_mask = (doc_ids == previous).astype(jnp.float32)
    tail_mask = (doc_ids == last).astype(jnp.float32)
    rate = decay_rate[:, :, None]
    carry_in_map = residue[:, :, None] * jnp.exp(-rate * (place + 1.0)) * alive_mask
    carry_out_map = jnp.exp(-rate * (length - 1.0 - place)) * tail_mask
    back_out_map = jnp.exp(-rate * place) * alive_mask
    back_in_map = residue[:, :, None] * jnp.exp(-rate * (length - place)) * tail_mask
    steps_ahead = me - 1 - blocks
    joined_ahead = (steps_ahead >= 0) & (last_ids == previous)
    ahead_weight = jnp.where(
        joined_ahead[:, None, None],
        jnp.exp(
            -decay_rate[None]
            * (length * jnp.maximum(steps_ahead, 0)).astype(jnp.float32)[:, None, None]
        ),
        0.0,
    )
    steps_back = blocks - 1 - me
    before_ids = jnp.concatenate([jnp.full((1,), -1, jnp.int32), last_ids[:-1]])
    joined_back = (steps_back >= 0) & (before_ids == last)
    back_weight = jnp.where(
        joined_back[:, None, None],
        jnp.exp(
            -decay_rate[None]
            * (length * jnp.maximum(steps_back, 0)).astype(jnp.float32)[:, None, None]
        ),
        0.0,
    )
    key_f = key_input.astype(jnp.float32)
    value_f = value_input.astype(jnp.float32)
    query_f = query_input.astype(jnp.float32)
    mixed = (key_f * value_f).reshape(groups, group_rows, length)
    forward_part = jnp.einsum("gnl,gcl->gnc", carry_out_map, mixed, precision=HIGH)
    forward_all = lax.all_gather(forward_part, "ctx", axis=0)
    entering = jnp.sum(ahead_weight[..., None] * forward_all, axis=0)
    partial_grad = lax.dot_general(
        out_weight, out_cotangent, (((1,), (1,)), ((), ())), preferred_element_type=jnp.float32
    )
    output_grad = lax.psum_scatter(partial_grad, "ch", scatter_dimension=0, tiled=True)
    kernel = local_kernel(decay_rate, residue, doc_ids, length)
    filtered = jnp.einsum("gcs,gts->gct", mixed, kernel, precision=HIGH)
    filtered = filtered + jnp.einsum("gnc,gnt->gct", entering, carry_in_map, precision=HIGH)
    filtered = filtered.reshape(rows_here, length)
    gated = (query_f * filtered).astype(jnp.bfloat16)
    gated_rows = exchange_rows(gated, n_ctx, n_ch)
    signal = (output_grad * query_f).reshape(groups, group_rows, length)
    backward_part = jnp.einsum("gnl,gcl->gnc", back_out_map, signal, precision=HIGH)
    backward_all = lax.all_gather(backward_part, "ctx", axis=0)
    query_grad = (output_grad * filtered).astype(jnp.bfloat16)
    spread = jnp.einsum("gct,gts->gcs", signal, kernel, precision=HIGH)
    returning = jnp.sum(back_weight[..., None] * backward_all, axis=0)
    spread = spread + jnp.einsum("gnc,gns->gcs", returning, back_in_map, precision=HIGH)
    spread = spread.reshape(rows_here, length)
    key_grad = (spread * value_f).astype(jnp.bfloat16)
    value_grad = (spread * key_f).astype(jnp.bfloat16)
    norm_factor = 1.0 / math.sqrt(length * n_ctx)
    weight_grad = (
        jnp.dot(gated_rows, cotangent_all, preferred_element_type=jnp.float32) * norm_factor
    )
    return (query_grad, key_grad, value_grad, weight_grad)


def solution(mesh):
    return jax.shard_map(
        local,
        mesh=mesh,
        in_specs=(
            P("ch", "ctx"),
            P("ch", "ctx"),
            P("ch", "ctx"),
            P("ch", None),
            P("ch", None),
            P(),
            P(None, "ch"),
            P("ctx", "ch"),
        ),
        out_specs=(P("ch", "ctx"), P("ch", "ctx"), P("ch", "ctx"), P("ctx", "ch")),
        check_vma=False,
    )
```

profile of v0, /device:TPU:0, one launch (start us, length us, event | category | flops | bytes accessed | tf_op | source)
XLA Modules:
  0.0 227.6 jit_solution(17652264326971221755)
XLA Ops:
  8.0 0.0 reduce-scatter.2.cloned.1.call-start
  8.0 11.4 %fusion.67 = f32[4096,512]{1,0:T(8,128)} fusion(bf16[4096,1024]{1,0:T(8,128)(2,1)} %param.14, bf16[512,1024]{1,0:T(8,128)(2,1)} %param.15), kind=kOutput, calls=%fused_computation.103 | convolution fusion | flops 4294967296 | bytes 17825792 | tf_op jit(solution)/shard_map/dot_general | solution.py:95
  19.5 0.0 reduce-scatter.2.cloned.1.call-update
  19.5 0.0 copy-start.18
  19.5 0.0 copy-start
  19.5 0.0 copy-start.2
  19.5 0.0 all-gather.7.cloned.1.call-start
  19.6 0.5 all-gather.7.cloned.1.call-update
  20.1 0.0 all-gather.5.cloned.1.call-start
  20.2 0.7 fusion.28
  20.9 0.0 copy-start.4
  21.0 0.0 copy-start.7
  21.1 0.1 convert_reduce_fusion
  21.2 0.6 slice.18
  21.8 0.6 fusion.56
  23.1 0.1 convert_reduce_fusion.1
  23.2 0.7 compare_and_fusion
  23.9 0.6 compare_convert_fusion
  24.6 0.1 exponential_select_fusion
  24.7 0.0 copy-done
  24.7 0.3 convert_multiply_fusion.3
  25.0 0.9 fusion.24
  25.9 35.0 %all-gather = f32[16,16,512]{2,1,0:T(8,128)S(1)} all-gather(f32[2,16,512]{2,1,0:T(8,128)S(1)} %fusion.24), channel_id=2, replica_groups=mesh['ctx'=8,'ch'=4] {'ctx'}, dimensions={0}, use_global_device_ids=true | all-gather | bytes 589824 | tf_op jit(solution)/shard_map/all_gather | solution.py:93
  60.9 0.1 multiply_reduce_fusion.1
  61.0 0.2 fusion.7
  61.3 0.0 copy-start.15
  61.3 1.9 fusion.10
  63.2 0.0 copy-start.6
  63.2 2.4 %convolution_add_fusion.1 = f32[2,512,512]{2,1,0:T(8,128)} fusion(f32[2,512,512]{2,1,0:T(8,128)S(1)} %fusion.10, f32[2,16,512]{2,1,0:T(8,128)S(1)} %multiply_reduce_fusion.1, f32[512]{0:T(512)S(1)} %get-tuple-element.9, f32[512]{0:T(512)S(1)} %fusion.54, f32[2,16]{1,0:T(2,128)S(1)} %copy-done.15, f32[2,16]{1,0:T(2,128)S(1)} %neg.5), kind=kOutput, calls=%fused_computation.22 | convolution fusion | flops 50905088 | bytes 4264192 | tf_op jit(solution)/shard_map/gnc,gnt->gct/dot_general | solution.py:101
  65.6 28.5 %reduce-scatter.2.cloned.1.call-done = f32[1024,512]{1,0:T(8,128)} async-done(((f32[4096,512]{1,0:T(8,128)}), f32[1024,512]{1,0:T(8,128)}) %reduce-scatter.2.cloned.1.call-update) | async-done | bytes 2097168 | tf_op jit(solution)/shard_map/reduce_scatter | solution.py:98
  94.1 3.9 %fusion.2 = (bf16[1024,512]{1,0:T(8,128)(2,1)S(1)}, bf16[1024,512]{1,0:T(8,128)(2,1)}, f32[1024,512]{1,0:T(8,128)S(1)}) fusion(bf16[1024,512]{1,0:T(8,128)(2,1)S(1)} %copy-done.6, f32[2,512,512]{2,1,0:T(8,128)} %convolution_add_fusion.1, f32[1024,512]{1,0:T(8,128)} %reduce-scatter.2.cloned.1.call-done), kind=kLoop, calls=%fused_computation.11 | loop fusion | flops 3145728 | bytes 9437184 | tf_op jit(solution)/shard_map/convert_element_type | solution.py:103
  98.0 0.1 copy.24
  98.1 16.9 %all_to_all.20 = bf16[2,4,128,512]{3,2,0,1:T(8,128)(2,1)S(1)} all-to-all(bf16[2,4,128,512]{3,2,0,1:T(8,128)(2,1)S(1)} %copy.24), channel_id=1, replica_groups=mesh['ctx'=8,'ch'=4] {'ch'}, dimensions={1} | all-to-all | bytes 2097152 | tf_op jit(solution)/shard_map/all_to_all | solution.py:37
  115.0 54.5 %all_to_all.21 = bf16[8,128,512]{2,1,0:T(8,128)(2,1)S(1)} all-to-all(bf16[8,128,512]{2,1,0:T(8,128)(2,1)S(1)} %bitcast.38), channel_id=1, replica_groups=mesh['ctx'=8,'ch'=4] {'ctx'}, dimensions={0} | all-to-all | bytes 2097152 | tf_op jit(solution)/shard_map/all_to_all | solution.py:39
  169.5 1.3 copy.25
  170.8 0.0 all-gather.5.cloned.1.call-update
  170.9 1.7 fusion.16
  172.6 31.6 %all-gather.1 = f32[16,16,512]{2,1,0:T(8,128)S(1)} all-gather(f32[2,16,512]{2,1,0:T(8,128)S(1)} %fusion.16), channel_id=3, replica_groups=mesh['ctx'=8,'ch'=4] {'ctx'}, dimensions={0}, use_global_device_ids=true | all-gather | bytes 589824 | tf_op jit(solution)/shard_map/all_gather | solution.py:107
  204.2 0.1 multiply_reduce_fusion
  204.3 0.0 copy-start.16
  204.4 1.9 fusion.8
  206.3 0.0 copy-start.1
  206.3 0.0 copy-start.3
  206.3 1.0 convolution_add_fusion
  207.3 0.1 copy-done.1
  207.5 0.3 copy-done.3
  207.8 1.9 fusion
  209.7 10.5 %convolution_multiply_fusion = f32[512,1024]{1,0:T(8,128)} fusion(bf16[512,4096]{0,1:T(8,128)(2,1)} %all-gather.5.cloned.1.call-done, bf16[4096,1024]{1,0:T(8,128)(2,1)} %all-gather.7.cloned.1.call-done), kind=kOutput, calls=%fused_computation.23 | convolution fusion | flops 4295491584 | bytes 14680064 | tf_op jit(solution)/shard_map/dot_general | solution.py:117
  (40 shorter events, 0.2 us)
Async XLA Ops:
  8.0 86.1 %reduce-scatter.2.cloned.1.call-start = ((), (), s32[]{:S(2)}) async-start(), calls=%async_computation.3 | async-start | bytes 10485760 | tf_op jit(solution)/shard_map/reduce_scatter | solution.py:98
  19.5 0.7 copy-start.17
  19.5 0.7 copy-start.14
  19.5 1.6 copy-start.18
  19.5 5.2 %copy-start = (bf16[1024,512]{1,0:T(8,128)(2,1)S(1)}, bf16[1024,512]{1,0:T(8,128)(2,1)}, u32[]{:S(2)}) copy-start(bf16[1024,512]{1,0:T(8,128)(2,1)} %param.10) | copy-start | bytes 3145732
  19.5 5.2 %copy-start.2 = (bf16[1024,512]{1,0:T(8,128)(2,1)S(1)}, bf16[1024,512]{1,0:T(8,128)(2,1)}, u32[]{:S(2)}) copy-start(bf16[1024,512]{1,0:T(8,128)(2,1)} %param.9) | copy-start | bytes 3145732
  19.5 190.1 %all-gather.7.cloned.1.call-start = ((), (), s32[]{:S(2)}) async-start(), calls=%async_computation.5 | async-start | bytes 9437184 | tf_op jit(solution)/shard_map/all_gather | solution.py:59
  20.1 189.6 %all-gather.5.cloned.1.call-start = ((), (), s32[]{:S(2)}) async-start(), calls=%async_computation.4 | async-start | bytes 5242880 | tf_op jit(solution)/shard_map/all_gather | solution.py:41
  20.9 40.3 %copy-start.4 = (f32[2,512,128]{1,2,0:T(8,128)}, f32[2,512,128]{1,2,0:T(8,128)S(1)}, u32[]{:S(2)}) copy-start(f32[2,512,128]{1,2,0:T(8,128)S(1)} %fusion.28) | copy-start | bytes 1572868
  21.0 40.3 %copy-start.11 = (f32[2,128,128]{1,2,0:T(8,128)}, f32[2,128,128]{1,2,0:T(8,128)S(1)}, u32[]{:S(2)}) copy-start(f32[2,128,128]{1,2,0:T(8,128)S(1)} %slice.22) | copy-start | bytes 393220
  21.0 40.3 %copy-start.7 = (f32[2,256,128]{1,2,0:T(8,128)}, f32[2,256,128]{1,2,0:T(8,128)S(1)}, u32[]{:S(2)}) copy-start(f32[2,256,128]{1,2,0:T(8,128)S(1)} %slice.21) | copy-start | bytes 786436
  24.6 38.6 %copy-start.13 = (f32[512]{0:T(512)}, f32[512]{0:T(512)S(1)}, u32[]{:S(2)}) copy-start(f32[512]{0:T(512)S(1)} %get-tuple-element.9) | copy-start | bytes 6148
  61.3 1.9 copy-start.9
  61.3 1.9 copy-start.15
  63.2 30.9 %copy-start.6 = (bf16[1024,512]{1,0:T(8,128)(2,1)S(1)}, bf16[1024,512]{1,0:T(8,128)(2,1)}, u32[]{:S(2)}) copy-start(bf16[1024,512]{1,0:T(8,128)(2,1)} %param.8) | copy-start | bytes 3145732
  170.8 33.5 %copy-start.5 = (f32[2,512,128]{1,2,0:T(8,128)S(1)}, f32[2,512,128]{1,2,0:T(8,128)}, u32[]{:S(2)}) copy-start(f32[2,512,128]{1,2,0:T(8,128)} %copy-done.4) | copy-start | bytes 1572868
  170.8 33.5 %copy-start.8 = (f32[2,256,128]{1,2,0:T(8,128)S(1)}, f32[2,256,128]{1,2,0:T(8,128)}, u32[]{:S(2)}) copy-start(f32[2,256,128]{1,2,0:T(8,128)} %copy-done.7) | copy-start | bytes 786436
  170.8 33.5 %copy-start.12 = (f32[2,128,128]{1,2,0:T(8,128)S(1)}, f32[2,128,128]{1,2,0:T(8,128)}, u32[]{:S(2)}) copy-start(f32[2,128,128]{1,2,0:T(8,128)} %copy-done.11) | copy-start | bytes 393220
  170.8 33.5 %copy-start.10 = (pred[512,512]{0,1:T(8,128)(4,1)S(1)}, pred[512,512]{0,1:T(8,128)(4,1)}, u32[]{:S(2)}) copy-start(pred[512,512]{0,1:T(8,128)(4,1)} %copy-done.9) | copy-start | bytes 786436
  204.3 1.9 copy-start.16
  206.3 1.2 copy-start.1
  206.3 1.5 copy-start.3
Sparse Core Ops, SparseCore 0:
  19.6 74.4 reduce-scatter.1
Sparse Core Ops, SparseCore 1:
  22.4 151.2 all-gather.6
  175.7 33.9 all-gather.4
where the time goes:
time: 228 us
  blocking collectives  138 us (61%)
  matrix products  32.5 us (14%)
  waiting for transfers between devices  29.1 us (13%)
  between operations  16.6 us (7%)
  other arithmetic  8.81 us (4%)
  local copies, waits for them, and re-layouts  2.62 us (1%)
    all_to_all x1, blocking collectives, exchange_rows(): lax.all_to_all(pieces, 'ctx', split_axis=0, concat_axis=0, tiled=True)  54.5 us
    all_gather x1, blocking collectives, local(): forward_all = lax.all_gather(forward_part, 'ctx', axis=0)  35 us
    all_gather x1, blocking collectives, local(): backward_all = lax.all_gather(backward_part, 'ctx', axis=0)  31.6 us
    reduce_scatter x1, waiting for transfers between devices, local(): lax.psum_scatter(partial_grad, 'ch', scatter_dimension=0, tiled=True)  28.5 us
    all_to_all x1, blocking collectives, exchange_rows(): lax.all_to_all(pieces, 'ch', split_axis=1, concat_axis=0, tiled=True)  16.9 us
    dot_general x1, matrix products, local(): lax.dot_general(out_weight, out_cotangent, (((1,), (1,)), ((), ())), pref...  11.4 us
    dot_general x1, matrix products, local(): jnp.dot(gated_rows, cotangent_all, preferred_element_type=jnp.float32)  10.5 us
  transfers between devices with their start and end apart: 3, of which 1 were waited for; matrix products, arithmetic and copies ran while one was open for 9% of the time, Pallas kernels for 0%

commit v1 on v0

--- a/solution.py
+++ b/solution.py
@@ -6,6 +6,17 @@
 
 HIGH = lax.Precision.HIGH
 TILE = 128
+
+
+def split_up(value, dim, devices):
+    before, after = (value.shape[:dim], value.shape[dim + 1 :])
+    return jnp.moveaxis(value.reshape(*before, devices, -1, *after), dim, 0)
+
+
+def in_order(parts, dim):
+    lengths = list(parts.shape[1:])
+    lengths[dim] *= parts.shape[0]
+    return jnp.moveaxis(parts, 0, dim).reshape(lengths)
 
 
 def doc_of(doc_ends, positions):
@@ -34,7 +45,14 @@
     rows, length = gated.shape
     mine = rows * n_ch // n_ctx
     pieces = gated.reshape(n_ctx // n_ch, n_ch, mine // n_ch, length)
-    pieces = lax.all_to_all(pieces, "ch", split_axis=1, concat_axis=0, tiled=True)
+    size, index = (lax.axis_size("ch"), lax.axis_index("ch"))
+    blocks_2 = split_up(pieces, 1, size)
+    gathered = [blocks_2[index]]
+    for turn in range(1, size):
+        sent = blocks_2[index ^ turn]
+        gathered.append(lax.ppermute(sent, "ch", [(i, i ^ turn) for i in range(size)]))
+    blocks_2 = jnp.stack(gathered)[index ^ jnp.arange(size)]
+    pieces = in_order(blocks_2, 0)
     pieces = pieces.reshape(n_ctx, mine // n_ch, length)
     pieces = lax.all_to_all(pieces, "ctx", split_axis=0, concat_axis=0, tiled=True)
     pieces = pieces.transpose(1, 0, 2).reshape(mine // n_ch, n_ctx * length)

time: 228 us -> 227 us (level)
  blocking collectives: 138 us -> 120 us
  waiting for transfers between devices: 29.1 us -> 41.4 us
    all_to_all x1 -> x0, blocking collectives: 16.9 us -> none  [exchange_rows(): lax.all_to_all(pieces, 'ch', split_axis=1, concat_axis=0, tiled=True)]
    ppermute x0 -> x3, waiting for transfers between devices: none -> 11.7 us  [exchange_rows(): lax.ppermute(sent, 'ch', [(i, i ^ turn) for i in range(size)])]
  transfers between devices with their start and end apart: 3 -> 6, of which waited for: 1 -> 4; matrix products, arithmetic and copies ran while one was open for 9% -> 11% of each run, Pallas kernels for 0% -> 0%
where the time goes in v1:
time: 227 us
  blocking collectives  120 us (53%)
  waiting for transfers between devices  41.4 us (18%)
  matrix products  32.4 us (14%)
  between operations  16.6 us (7%)
  other arithmetic  9.61 us (4%)
  local copies, waits for them, and re-layouts  4.63 us (2%)
    all_to_all x1, blocking collectives, exchange_rows(): lax.all_to_all(pieces, 'ctx', split_axis=0, concat_axis=0, tiled=True)  53.7 us
    all_gather x1, blocking collectives, local(): forward_all = lax.all_gather(forward_part, 'ctx', axis=0)  34.8 us
    all_gather x1, blocking collectives, local(): backward_all = lax.all_gather(backward_part, 'ctx', axis=0)  31.5 us
    reduce_scatter x1, waiting for transfers between devices, local(): lax.psum_scatter(partial_grad, 'ch', scatter_dimension=0, tiled=True)  28.5 us
    ppermute x3, waiting for transfers between devices, exchange_rows(): lax.ppermute(sent, 'ch', [(i, i ^ turn) for i in range(size)])  11.7 us
    dot_general x1, matrix products, local(): lax.dot_general(out_weight, out_cotangent, (((1,), (1,)), ((), ())), pref...  11.4 us
    dot_general x1, matrix products, local(): jnp.dot(gated_rows, cotangent_all, preferred_element_type=jnp.float32)  10.5 us
  transfers between devices with their start and end apart: 6, of which 4 were waited for; matrix products, arithmetic and copies ran while one was open for 11% of the time, Pallas kernels for 0%

profile of v1, /device:TPU:0, one launch (start us, length us, event | category | flops | bytes accessed | tf_op | source)
XLA Modules:
  0.0 226.9 jit_solution(4695350531853228166)
XLA Ops:
  8.0 0.0 reduce-scatter.2.cloned.1.call-start
  8.0 11.4 %fusion.68 = f32[4096,512]{1,0:T(8,128)} fusion(bf16[4096,1024]{1,0:T(8,128)(2,1)} %param.14, bf16[512,1024]{1,0:T(8,128)(2,1)} %param.15), kind=kOutput, calls=%fused_computation.112 | convolution fusion | flops 4294967296 | bytes 17825792 | tf_op jit(solution)/shard_map/dot_general | solution.py:113
  19.5 0.0 reduce-scatter.2.cloned.1.call-update
  19.5 0.0 copy-start
  19.5 0.0 copy-start.2
  19.5 0.0 all-gather.7.cloned.1.call-start
  19.6 0.5 all-gather.7.cloned.1.call-update
  20.1 0.0 all-gather.5.cloned.1.call-start
  20.2 0.7 fusion.28
  21.1 0.1 convert_reduce_fusion
  21.2 0.6 slice.18
  21.8 0.6 fusion.56
  23.1 0.1 convert_reduce_fusion.1
  23.2 0.7 compare_and_fusion
  23.9 0.6 compare_convert_fusion
  24.6 0.1 exponential_select_fusion
  24.7 0.3 convert_multiply_fusion.3
  25.0 1.0 fusion.24
  26.0 34.8 %all-gather = f32[16,16,512]{2,1,0:T(8,128)S(1)} all-gather(f32[2,16,512]{2,1,0:T(8,128)S(1)} %fusion.24), channel_id=2, replica_groups=mesh['ctx'=8,'ch'=4] {'ctx'}, dimensions={0}, use_global_device_ids=true | all-gather | bytes 589824 | tf_op jit(solution)/shard_map/all_gather | solution.py:111
  60.8 0.1 multiply_reduce_fusion.1
  60.9 0.2 fusion.7
  61.2 0.0 copy-start.15
  61.2 1.9 fusion.10
  63.2 2.4 %convolution_add_fusion.1 = f32[2,512,512]{2,1,0:T(8,128)} fusion(f32[2,512,512]{2,1,0:T(8,128)S(1)} %fusion.10, f32[2,16,512]{2,1,0:T(8,128)S(1)} %multiply_reduce_fusion.1, f32[512]{0:T(512)S(1)} %get-tuple-element.13, f32[512]{0:T(512)S(1)} %fusion.54, f32[2,16]{1,0:T(2,128)S(1)} %copy-done.15, f32[2,16]{1,0:T(2,128)S(1)} %neg.5), kind=kOutput, calls=%fused_computation.23 | convolution fusion | flops 50905088 | bytes 4264192 | tf_op jit(solution)/shard_map/gnc,gnt->gct/dot_general | solution.py:119
  65.6 28.5 %reduce-scatter.2.cloned.1.call-done = f32[1024,512]{1,0:T(8,128)} async-done(((f32[4096,512]{1,0:T(8,128)}), f32[1024,512]{1,0:T(8,128)}) %reduce-scatter.2.cloned.1.call-update) | async-done | bytes 2097168 | tf_op jit(solution)/shard_map/reduce_scatter | solution.py:116
  94.1 4.0 %fusion.2 = (bf16[1024,512]{1,0:T(8,128)(2,1)S(1)}, bf16[1024,512]{1,0:T(8,128)(2,1)}, f32[1024,512]{1,0:T(8,128)S(1)}) fusion(bf16[1024,512]{1,0:T(8,128)(2,1)S(1)} %copy-done.6, f32[2,512,512]{2,1,0:T(8,128)} %convolution_add_fusion.1, f32[1024,512]{1,0:T(8,128)} %reduce-scatter.2.cloned.1.call-done), kind=kLoop, calls=%fused_computation.12 | loop fusion | flops 3145728 | bytes 9437184 | tf_op jit(solution)/shard_map/convert_element_type | solution.py:121
  98.0 0.1 dynamic-slice_bitcast_fusion.3
  98.1 0.1 collective-permute-start.2
  98.2 1.4 collective-permute-start.1
  99.7 0.4 collective-permute-start
  100.1 0.6 pad_clamp_fusion
  100.7 6.1 %collective-permute-done.2 = bf16[2,1,128,512]{3,2,0,1:T(8,128)(2,1)S(1)} collective-permute-done((bf16[2,1,128,512]{3,2,0,1:T(8,128)(2,1)S(1)}, bf16[2,1,128,512]{3,2,0,1:T(8,128)(2,1)S(1)}, u32[]{:S(2)}, u32[]{:S(2)}) %collective-permute-start.2) | collective-permute-done | bytes 262176 | tf_op jit(solution)/shard_map/ppermute | solution.py:53
  106.8 5.6 %collective-permute-done.1 = bf16[2,1,128,512]{3,2,0,1:T(8,128)(2,1)S(1)} collective-permute-done((bf16[2,1,128,512]{3,2,0,1:T(8,128)(2,1)S(1)}, bf16[2,1,128,512]{3,2,0,1:T(8,128)(2,1)S(1)}, u32[]{:S(2)}, u32[]{:S(2)}) %collective-permute-start.1) | collective-permute-done | bytes 262176 | tf_op jit(solution)/shard_map/ppermute | solution.py:53
  112.4 0.1 maximum_bitcast_fusion
  112.5 1.7 gather_fusion
  114.3 1.6 copy.24
  115.9 53.7 %all_to_all.5 = bf16[8,128,512]{1,2,0:T(8,128)(2,1)} all-to-all(bf16[8,128,512]{1,2,0:T(8,128)(2,1)S(1)} %copy.24), channel_id=1, replica_groups=mesh['ctx'=8,'ch'=4] {'ctx'}, dimensions={0} | all-to-all | bytes 2097152 | tf_op jit(solution)/shard_map/all_to_all | solution.py:57
  169.6 0.0 all-gather.5.cloned.1.call-update
  169.7 1.6 fusion.16
  171.3 31.5 %all-gather.1 = f32[16,16,512]{2,1,0:T(8,128)S(1)} all-gather(f32[2,16,512]{2,1,0:T(8,128)S(1)} %fusion.16), channel_id=3, replica_groups=mesh['ctx'=8,'ch'=4] {'ctx'}, dimensions={0}, use_global_device_ids=true | all-gather | bytes 589824 | tf_op jit(solution)/shard_map/all_gather | solution.py:125
  202.8 0.1 multiply_reduce_fusion
  203.0 1.8 fusion.8
  204.9 1.0 convolution_add_fusion
  205.9 0.1 copy-done.1
  206.1 0.3 copy-done.3
  206.4 1.9 fusion
  208.3 0.7 all-gather.5.cloned.1.call-done
  209.0 10.5 %convolution_multiply_fusion = f32[512,1024]{1,0:T(8,128)} fusion(bf16[512,4096]{0,1:T(8,128)(2,1)} %all-gather.5.cloned.1.call-done, bf16[4096,1024]{1,0:T(8,128)(2,1)} %all-gather.7.cloned.1.call-done), kind=kOutput, calls=%fused_computation.24 | convolution fusion | flops 4295491584 | bytes 14680064 | tf_op jit(solution)/shard_map/dot_general | solution.py:135
  (49 shorter events, 0.2 us)
Async XLA Ops:
  8.0 86.1 %reduce-scatter.2.cloned.1.call-start = ((), (), s32[]{:S(2)}) async-start(), calls=%async_computation.2 | async-start | bytes 10485760 | tf_op jit(solution)/shard_map/reduce_scatter | solution.py:116
  19.5 0.7 copy-start.17
  19.5 0.7 copy-start.14
  19.5 1.6 copy-start.18
  19.5 5.2 %copy-start = (bf16[1024,512]{1,0:T(8,128)(2,1)S(1)}, bf16[1024,512]{1,0:T(8,128)(2,1)}, u32[]{:S(2)}) copy-start(bf16[1024,512]{1,0:T(8,128)(2,1)} %param.10) | copy-start | bytes 3145732
  19.5 5.2 %copy-start.2 = (bf16[1024,512]{1,0:T(8,128)(2,1)S(1)}, bf16[1024,512]{1,0:T(8,128)(2,1)}, u32[]{:S(2)}) copy-start(bf16[1024,512]{1,0:T(8,128)(2,1)} %param.9) | copy-start | bytes 3145732
  19.5 188.8 %all-gather.7.cloned.1.call-start = ((), (), s32[]{:S(2)}) async-start(), calls=%async_computation.4 | async-start | bytes 9437184 | tf_op jit(solution)/shard_map/all_gather | solution.py:77
  20.1 188.9 %all-gather.5.cloned.1.call-start = ((), (), s32[]{:S(2)}) async-start(), calls=%async_computation.3 | async-start | bytes 5242880 | tf_op jit(solution)/shard_map/all_gather | solution.py:59
  20.9 40.3 %copy-start.4 = (f32[2,512,128]{1,2,0:T(8,128)}, f32[2,512,128]{1,2,0:T(8,128)S(1)}, u32[]{:S(2)}) copy-start(f32[2,512,128]{1,2,0:T(8,128)S(1)} %fusion.28) | copy-start | bytes 1572868
  21.0 40.2 %copy-start.11 = (f32[2,128,128]{1,2,0:T(8,128)}, f32[2,128,128]{1,2,0:T(8,128)S(1)}, u32[]{:S(2)}) copy-start(f32[2,128,128]{1,2,0:T(8,128)S(1)} %slice.24) | copy-start | bytes 393220
  21.0 40.2 %copy-start.7 = (f32[2,256,128]{1,2,0:T(8,128)}, f32[2,256,128]{1,2,0:T(8,128)S(1)}, u32[]{:S(2)}) copy-start(f32[2,256,128]{1,2,0:T(8,128)S(1)} %slice.23) | copy-start | bytes 786436
  24.6 38.6 %copy-start.13 = (f32[512]{0:T(512)}, f32[512]{0:T(512)S(1)}, u32[]{:S(2)}) copy-start(f32[512]{0:T(512)S(1)} %get-tuple-element.13) | copy-start | bytes 6148
  61.2 1.9 copy-start.9
  61.2 2.0 copy-start.15
  63.2 30.9 %copy-start.6 = (bf16[1024,512]{1,0:T(8,128)(2,1)S(1)}, bf16[1024,512]{1,0:T(8,128)(2,1)}, u32[]{:S(2)}) copy-start(bf16[1024,512]{1,0:T(8,128)(2,1)} %param.8) | copy-start | bytes 3145732
  98.1 8.7 %collective-permute-start.2 = (bf16[2,1,128,512]{3,2,0,1:T(8,128)(2,1)S(1)}, bf16[2,1,128,512]{3,2,0,1:T(8,128)(2,1)S(1)}, u32[]{:S(2)}, u32[]{:S(2)}) collective-permute-start(bf16[2,1,128,512]{3,2,0,1:T(8,128)(2,1)S(1)} %get-tuple-element.10), channel_id=1, source_target_pairs={{0,3},{1,2},{2,1},{3,0},{4,7},{5,6},{6,5},{7,4},{8,11},{9,10},{10,... | collective-permute-start | bytes 786440 | tf_op jit(solution)/shard_map/ppermute | solution.py:53
  98.2 14.2 %collective-permute-start.1 = (bf16[2,1,128,512]{3,2,0,1:T(8,128)(2,1)S(1)}, bf16[2,1,128,512]{3,2,0,1:T(8,128)(2,1)S(1)}, u32[]{:S(2)}, u32[]{:S(2)}) collective-permute-start(bf16[2,1,128,512]{3,2,0,1:T(8,128)(2,1)S(1)} %get-tuple-element.11), channel_id=1, source_target_pairs={{0,2},{1,3},{2,0},{3,1},{4,6},{5,7},{6,4},{7,5},{8,10},{9,11},{10,... | collective-permute-start | bytes 786440 | tf_op jit(solution)/shard_map/ppermute | solution.py:53
  99.7 12.8 %collective-permute-start = (bf16[2,1,128,512]{3,2,0,1:T(8,128)(2,1)S(1)}, bf16[2,1,128,512]{3,2,0,1:T(8,128)(2,1)S(1)}, u32[]{:S(2)}, u32[]{:S(2)}) collective-permute-start(bf16[2,1,128,512]{3,2,0,1:T(8,128)(2,1)S(1)} %get-tuple-element.12), channel_id=1, source_target_pairs={{0,1},{1,0},{2,3},{3,2},{4,5},{5,4},{6,7},{7,6},{8,9},{9,8},{10,11... | collective-permute-start | bytes 786440 | tf_op jit(solution)/shard_map/ppermute | solution.py:53
  169.6 33.4 %copy-start.5 = (f32[2,512,128]{1,2,0:T(8,128)S(1)}, f32[2,512,128]{1,2,0:T(8,128)}, u32[]{:S(2)}) copy-start(f32[2,512,128]{1,2,0:T(8,128)} %copy-done.4) | copy-start | bytes 1572868
  169.6 33.4 %copy-start.8 = (f32[2,256,128]{1,2,0:T(8,128)S(1)}, f32[2,256,128]{1,2,0:T(8,128)}, u32[]{:S(2)}) copy-start(f32[2,256,128]{1,2,0:T(8,128)} %copy-done.7) | copy-start | bytes 786436
  169.6 33.4 %copy-start.12 = (f32[2,128,128]{1,2,0:T(8,128)S(1)}, f32[2,128,128]{1,2,0:T(8,128)}, u32[]{:S(2)}) copy-start(f32[2,128,128]{1,2,0:T(8,128)} %copy-done.11) | copy-start | bytes 393220
  169.6 33.4 %copy-start.10 = (pred[512,512]{0,1:T(8,128)(4,1)S(1)}, pred[512,512]{0,1:T(8,128)(4,1)}, u32[]{:S(2)}) copy-start(pred[512,512]{0,1:T(8,128)(4,1)} %copy-done.9) | copy-start | bytes 786436
  203.0 1.9 copy-start.16
  204.9 1.2 copy-start.1
  204.9 1.5 copy-start.3
Sparse Core Ops, SparseCore 0:
  19.6 74.4 reduce-scatter.1
Sparse Core Ops, SparseCore 1:
  22.3 151.2 all-gather.6
  175.1 33.8 all-gather.4
